TPU v7x, 128 devices: a whole 4x4x4 slice. The times are simulated.
128 devices in a mesh: seq: 64 (over z, y, x), exp: 2 (over core).
Axes of the slice: x: 4, y: 4, z: 4, core: 2. Of those that a mesh axis runs over, the one named last changes fastest.
Arguments:
- queries: bfloat16 [16384, 1024], P('seq', 'exp'), may hold values from -170 to 170
- keys: bfloat16 [16384, 1024], P('seq', 'exp'), may hold values from -5 to 5
- values: bfloat16 [16384, 1024], P('seq', 'exp'), may hold values from -6 to 6
- resid: bfloat16 [16384, 2048], P(('seq', 'exp')), may hold values from -6 to 6
- pair_ids: int32 [16384], replicated, may hold values from 0 to 63, never falling along the last dimension, each value on 1 to 512 neighbouring positions
- out_weight: bfloat16 [1024, 2048], P('exp'), may hold values from -0.1875 to 0.1875
- norm_gain: float32 [2048], replicated, may hold values from 0.5 to 1.5
- experts: int32 [16384, 6], P(('seq', 'exp')), may hold values from 0 to 63, all different within a row; in each aligned block of 128 rows (0 to 127, 128 to 255, ...) at most 24 rows name the same one
- gates: float32 [16384, 6], P(('seq', 'exp')), may hold values from 0.05 to 0.5
- w_gate: bfloat16 [64, 2048, 704], P('seq', None, 'exp'), may hold values from -0.125 to 0.125
- w_up: bfloat16 [64, 2048, 704], P('seq', None, 'exp'), may hold values from -0.125 to 0.125
- w_down: bfloat16 [64, 704, 2048], P('seq', 'exp'), may hold values from -0.21875 to 0.21875
Outputs:
- mixed: bfloat16 [16384, 2048], P(('seq', 'exp'))
Inputs may be any that keep to these rules, and one draw needn't show every extreme that they name: In the aligned blocks of 128 rows no expert is named more than 24 times, a bound that some block reaches; each row names 6 different experts. `pair_ids`: pair numbers never fall along the sequence; each pair has 1 to 512 tokens, one exactly that many.
All inputs are finite; a program needn't handle non-finite values.
Results may differ from a plain program's by a relative error of at most 0.012.
Values may be sent and summed in bfloat16 or wider, within the bound.
A program may use at most 128 MiB of HBM per device.

v0:
```python
import math
import jax
import jax.numpy as jnp
from jax import lax
from jax.sharding import PartitionSpec as P

HD = 128
TOP = 6


def with_halo(cells, sides, width):
    for axis, dim in sides:
        count = lax.axis_size(axis)
        ends = count - 1
        head = lax.slice_in_dim(cells, 0, width, axis=dim)
        tail = lax.slice_in_dim(cells, cells.shape[dim] - width, cells.shape[dim], axis=dim)
        cells = jnp.concatenate(
            [
                lax.ppermute(tail, axis, [(i, (i + 1) % count) for i in range(ends)]),
                cells,
                lax.ppermute(head, axis, [((i + 1) % count, i) for i in range(ends)]),
            ],
            axis=dim,
        )
    return cells


def send_back(result):
    return lax.all_to_all(result, "seq", split_axis=0, concat_axis=0, tiled=True)


def shards(
    queries,
    keys,
    values,
    resid,
    pair_ids,
    out_weight,
    norm_gain,
    experts,
    gates,
    w_gate,
    w_up,
    w_down,
):
    tok_rows = queries.shape[0]
    local_width = queries.shape[1]
    local_heads = local_width // HD
    shard = lax.axis_index("seq")
    stacked = jnp.stack([keys, values])
    widened = with_halo(stacked, (("seq", 1),), tok_rows)
    id_pad = jnp.pad(pair_ids, (tok_rows, tok_rows), constant_values=-1)
    key_ids = lax.dynamic_slice_in_dim(id_pad, shard * tok_rows, 3 * tok_rows, 0)
    query_ids = lax.dynamic_slice_in_dim(id_pad, shard * tok_rows + tok_rows, tok_rows, 0)
    query_pos = jnp.arange(tok_rows, dtype=jnp.int32) + tok_rows
    key_pos = jnp.arange(3 * tok_rows, dtype=jnp.int32)
    allowed = (query_ids[:, None] == key_ids[None, :]) & (
        jnp.abs(query_pos[:, None] - key_pos[None, :]) < tok_rows
    )
    query_heads = queries.reshape(tok_rows, local_heads, HD)
    key_heads = widened[0].reshape(3 * tok_rows, local_heads, HD)
    value_heads = widened[1].reshape(3 * tok_rows, local_heads, HD)
    score = jnp.einsum(
        "qhd,khd->hqk", query_heads, key_heads, preferred_element_type=jnp.float32
    ) / math.sqrt(HD)
    score = jnp.where(allowed[None], score, -jnp.inf)
    top = jnp.max(score, axis=-1, keepdims=True)
    weights = jnp.exp(score - top)
    probs = (weights / jnp.sum(weights, axis=-1, keepdims=True)).astype(jnp.bfloat16)
    attended = jnp.einsum("hqk,khd->qhd", probs, value_heads, preferred_element_type=jnp.float32)
    attended = attended.reshape(tok_rows, local_width).astype(jnp.bfloat16)
    moe_rows = resid.shape[0]
    projected = lax.psum(
        jnp.dot(attended, out_weight, preferred_element_type=jnp.float32).astype(jnp.bfloat16),
        "exp",
    ).astype(jnp.float32)
    projected = lax.dynamic_slice_in_dim(projected, lax.axis_index("exp") * moe_rows, moe_rows, 0)
    stream = resid.astype(jnp.float32) + projected
    meansq = jnp.mean(stream * stream, axis=-1, keepdims=True)
    normed = (stream * lax.rsqrt(meansq + 1e-05) * norm_gain).astype(jnp.bfloat16)
    n_experts = lax.axis_size("seq") * w_gate.shape[0]
    capacity = 2 * moe_rows * TOP // n_experts
    flat_experts = experts.reshape(-1)
    onehot = (flat_experts[:, None] == jnp.arange(n_experts, dtype=jnp.int32)[None, :]).astype(
        jnp.int32
    )
    ranks = jnp.cumsum(onehot, axis=0) - onehot
    slot_index = jnp.sum(ranks * onehot, axis=1)
    destination = flat_experts * capacity + slot_index
    token_of = jnp.arange(moe_rows * TOP, dtype=jnp.int32) // TOP
    outgoing = (
        jnp.zeros((n_experts * capacity, normed.shape[1]), jnp.bfloat16)
        .at[destination]
        .set(normed[token_of])
    )
    outgoing = outgoing.reshape(n_experts, capacity, normed.shape[1])
    arrived = lax.all_to_all(outgoing, "seq", split_axis=0, concat_axis=0, tiled=True)
    sources = arrived.shape[0]
    slots = arrived.shape[1]
    inputs = arrived.reshape(sources * slots, arrived.shape[2])
    group = lax.all_gather(inputs, "exp", axis=0, tiled=True)
    gate_part = jnp.dot(group, w_gate[0], preferred_element_type=jnp.float32)
    up_part = jnp.dot(group, w_up[0], preferred_element_type=jnp.float32)
    act = (jax.nn.silu(gate_part) * up_part).astype(jnp.bfloat16)
    result = lax.psum_scatter(
        jnp.dot(act, w_down[0], preferred_element_type=jnp.float32).astype(jnp.bfloat16),
        "exp",
        scatter_dimension=0,
        tiled=True,
    )
    result = result.reshape(sources, slots, result.shape[1])
    back = send_back(result)
    gathered = back.reshape(n_experts * capacity, back.shape[2])[destination]
    gathered = gathered.reshape(moe_rows, TOP, gathered.shape[1]).astype(jnp.float32)
    mixture = jnp.einsum("mk,mkd->md", gates, gathered)
    return (stream + mixture).astype(jnp.bfloat16)


def solution(mesh):
    in_specs = (
        P("seq", "exp"),
        P("seq", "exp"),
        P("seq", "exp"),
        P(("seq", "exp"), None),
        P(),
        P("exp", None),
        P(),
        P(("seq", "exp"), None),
        P(("seq", "exp"), None),
        P("seq", None, "exp"),
        P("seq", None, "exp"),
        P("seq", "exp", None),
    )
    out_specs = P(("seq", "exp"), None)
    return jax.shard_map(shards, mesh=mesh, in_specs=in_specs, out_specs=out_specs, check_vma=False)
```

profile of v0, /device:TPU:10, one launch (start us, length us, event | category | flops | bytes accessed | tf_op | source)
XLA Modules:
  0.0 383.7 jit_solution(15358219397726013312)
XLA Ops:
  6.5 1.2 copy.16
  8.9 3.4 collective-permute-start
  12.3 2.4 collective-permute-start.1
  16.6 7.9 %collective-permute-done = bf16[2,256,512]{1,2,0:T(8,128)(2,1)} collective-permute-done((bf16[2,256,512]{1,2,0:T(8,128)(2,1)S(1)}, bf16[2,256,512]{1,2,0:T(8,128)(2,1)}, u32[]{:S(2)}, u32[]{:S(2)}) %collective-permute-start) | collective-permute-done | bytes 524320 | tf_op jit(solution)/shard_map/ppermute | solution.py:19
  24.6 3.1 collective-permute-done.1
  27.7 1.3 pad_maximum_fusion
  29.8 1.6 fusion.32
  31.8 1.7 convolution_convert_fusion.1
  34.1 1.8 reduce-window.6
  36.6 28.0 %all-reduce.3.cloned.1.call-done = bf16[256,2048]{1,0:T(8,128)(2,1)} async-done(((bf16[256,2048]{1,0:T(8,128)(2,1)}), bf16[256,2048]{1,0:T(8,128)(2,1)}) %all-reduce.3.cloned.1.call-update) | async-done | bytes 1048592 | tf_op jit(solution)/shard_map/psum | solution.py:73
  64.6 1.3 multiply_reduce_fusion
  65.9 1.3 multiply_convert_fusion
  67.2 24.2 %scatter_custom_fusion = bf16[1536,2048]{1,0:T(8,128)(2,1)} fusion(s32[768]{0:T(1024)S(1)} %fusion.26, bf16[128,2048]{1,0:T(8,128)(2,1)S(1)} %multiply_convert_fusion, s32[1024]{0:T(1024)S(1)} %pad_clamp_fusion.1, bf16[]{:T(256)} %constant.50.clone.1), kind=kCustom, calls=%fused_computation.8 | custom fusion | bytes 6291458 | tf_op jit(solution)/shard_map/scatter | solution.py:94
  91.4 84.0 %all_to_all.10 = bf16[64,24,2048]{2,1,0:T(8,128)(2,1)} all-to-all(bf16[64,24,2048]{2,1,0:T(8,128)(2,1)} %bitcast.73), channel_id=1, replica_groups=mesh['seq'=64,'exp'=2] {'seq'}, dimensions={0} | all-to-all | bytes 12582912 | tf_op jit(solution)/shard_map/all_to_all | solution.py:97
  175.4 26.4 %all-gather.2.cloned.1.call-done = bf16[3072,2048]{1,0:T(8,128)(2,1)} async-done(((bf16[1536,2048]{1,0:T(8,128)(2,1)}), bf16[3072,2048]{1,0:T(8,128)(2,1)}) %all-gather.2.cloned.1.call-update) | async-done | bytes 12582928 | tf_op jit(solution)/shard_map/all_gather | solution.py:101
  201.8 9.8 %fusion.14 = f32[3072,352]{0,1:T(8,128)} fusion(bf16[3072,2048]{1,0:T(8,128)(2,1)} %all-gather.2.cloned.1.call-done, bf16[1,2048,352]{1,2,0:T(8,128)(2,1)S(1)} %copy-done.8), kind=kOutput, calls=%fused_computation.23 | convolution fusion | flops 4429185024 | bytes 18350080 | tf_op jit(solution)/shard_map/dot_general | solution.py:102
  211.6 18.6 %convolution_convert_fusion = bf16[3072,2048]{1,0:T(8,128)(2,1)} fusion(bf16[3072,2048]{1,0:T(8,128)(2,1)} %all-gather.2.cloned.1.call-done, f32[3072,352]{0,1:T(8,128)} %fusion.14, bf16[1,352,2048]{2,1,0:T(8,128)(2,1)} %param.23, bf16[1,2048,352]{1,2,0:T(8,128)(2,1)} %param.22), kind=kOutput, calls=%fused_computation.4 | convolution fusion | flops 8871149568 | bytes 32374784 | tf_op jit(solution)/shard_map/dot_general | solution.py:106
  230.2 25.7 %reduce-scatter.2.cloned.1.call-done = bf16[1536,2048]{1,0:T(8,128)(2,1)} async-done(((bf16[3072,2048]{1,0:T(8,128)(2,1)}), bf16[1536,2048]{1,0:T(8,128)(2,1)}) %reduce-scatter.2.cloned.1.call-update) | async-done | bytes 6291472 | tf_op jit(solution)/shard_map/reduce_scatter | solution.py:105
  255.9 10.7 %all-to-all-start.1 = ((bf16[64,24,2048]{2,1,0:T(8,128)(2,1)}), bf16[64,24,2048]{2,1,0:T(8,128)(2,1)}, u32[]{:S(2)}, u32[]{:S(2)}) async-start(bf16[64,24,2048]{2,1,0:T(8,128)(2,1)} %bitcast.74), calls=%async_computation.2 | async-start | bytes 12582912 | tf_op jit(solution)/shard_map/all_to_all | solution.py:29
  266.8 88.4 %all-to-all-done.1 = bf16[64,24,2048]{2,1,0:T(8,128)(2,1)} async-done(((bf16[64,24,2048]{2,1,0:T(8,128)(2,1)}), bf16[64,24,2048]{2,1,0:T(8,128)(2,1)}, u32[]{:S(2)}, u32[]{:S(2)}) %all-to-all-start.1) | async-done | bytes 6291488 | tf_op jit(solution)/shard_map/all_to_all | solution.py:29
  355.2 10.8 %gather_fusion = bf16[768,2048]{1,0:T(8,128)(2,1)} fusion(bf16[1536,2048]{1,0:T(8,128)(2,1)} %bitcast.14, s32[1024]{0:T(1024)S(1)} %pad_clamp_fusion), kind=kCustom, calls=%fused_computation.1 | custom fusion | bytes 6294528 | tf_op jit(solution)/shard_map/gather | solution.py:113
  365.9 6.4 %reshape.179 = bf16[128,6,2048]{2,1,0:T(8,128)(2,1)} reshape(bf16[768,2048]{1,0:T(8,128)(2,1)} %gather_fusion) | data formatting | bytes 6291456 | tf_op jit(solution)/shard_map/reshape | solution.py:114
  372.4 3.5 fusion.33
  375.9 1.3 fusion.17
  (48 shorter events, 5.6 us)
Async XLA Ops:
  6.5 25.3 %copy-start = (bf16[512,2048]{1,0:T(8,128)(2,1)S(1)}, bf16[512,2048]{1,0:T(8,128)(2,1)}, u32[]{:S(2)}) copy-start(bf16[512,2048]{1,0:T(8,128)(2,1)} %param.17) | copy-start | bytes 6291460
  6.5 58.0 %all-reduce.3.cloned.1.call-start = ((), (), s32[]{:S(2)}) async-start(), calls=%async_computation.3 | async-start | bytes 2097152 | tf_op jit(solution)/shard_map/psum | solution.py:73
  8.9 15.7 %collective-permute-start = (bf16[2,256,512]{1,2,0:T(8,128)(2,1)S(1)}, bf16[2,256,512]{1,2,0:T(8,128)(2,1)}, u32[]{:S(2)}, u32[]{:S(2)}) collective-permute-start(bf16[2,256,512]{1,2,0:T(8,128)(2,1)S(1)} %pad_maximum_fusion.1), channel_id=1, source_target_pairs={{0,2},{2,4},{4,6},{6,8},{8,10},{10,12},{12,14},{14,16},{16,18},{18... | collective-permute-start | bytes 1572872 | tf_op jit(solution)/shard_map/ppermute | solution.py:19
  12.3 15.4 %collective-permute-start.1 = (bf16[2,256,512]{1,2,0:T(8,128)(2,1)S(1)}, bf16[2,256,512]{1,2,0:T(8,128)(2,1)}, u32[]{:S(2)}, u32[]{:S(2)}) collective-permute-start(bf16[2,256,512]{1,2,0:T(8,128)(2,1)S(1)} %pad_maximum_fusion.1), channel_id=1, source_target_pairs={{2,0},{4,2},{6,4},{8,6},{10,8},{12,10},{14,12},{16,14},{18,16},{20... | collective-permute-start | bytes 1572872 | tf_op jit(solution)/shard_map/ppermute | solution.py:21
  16.6 12.5 %copy-start.4 = (bf16[256,512]{1,0:T(8,128)(2,1)S(1)}, bf16[256,512]{1,0:T(8,128)(2,1)}, u32[]{:S(2)}) copy-start(bf16[256,512]{1,0:T(8,128)(2,1)} %param.12) | copy-start | bytes 786436
  31.8 1.9 copy-start.5
  31.8 32.8 %copy-start.2 = (bf16[128,2048]{1,0:T(8,128)(2,1)S(1)}, bf16[128,2048]{1,0:T(8,128)(2,1)}, u32[]{:S(2)}) copy-start(bf16[128,2048]{1,0:T(8,128)(2,1)} %param.15) | copy-start | bytes 1572868
  31.8 34.1 %copy-start.6 = (f32[2048]{0:T(1024)S(1)}, f32[2048]{0:T(1024)}, u32[]{:S(2)}) copy-start(f32[2048]{0:T(1024)} %param.18) | copy-start | bytes 24580
  33.6 168.2 %all-gather.2.cloned.1.call-start = ((), (), s32[]{:S(2)}) async-start(), calls=%async_computation.4 | async-start | bytes 18874368 | tf_op jit(solution)/shard_map/all_gather | solution.py:101
  175.3 26.5 %copy-start.8 = (bf16[1,2048,352]{1,2,0:T(8,128)(2,1)S(1)}, bf16[1,2048,352]{1,2,0:T(8,128)(2,1)}, u32[]{:S(2)}) copy-start(bf16[1,2048,352]{1,2,0:T(8,128)(2,1)} %param.21) | copy-start | bytes 4325380
  175.4 80.5 %reduce-scatter.2.cloned.1.call-start = ((), (), s32[]{:S(2)}) async-start(), calls=%async_computation.5 | async-start | bytes 18874368 | tf_op jit(solution)/shard_map/reduce_scatter | solution.py:105
  255.9 10.7 %copy-start.7 = (f32[128,6]{0,1:T(8,128)S(1)}, f32[128,6]{0,1:T(8,128)}, u32[]{:S(2)}) copy-start(f32[128,6]{0,1:T(8,128)} %param.20) | copy-start | bytes 9220
  255.9 99.3 %all-to-all-start.1 = ((bf16[64,24,2048]{2,1,0:T(8,128)(2,1)}), bf16[64,24,2048]{2,1,0:T(8,128)(2,1)}, u32[]{:S(2)}, u32[]{:S(2)}) async-start(bf16[64,24,2048]{2,1,0:T(8,128)(2,1)} %bitcast.74), calls=%async_computation.2 | async-start | bytes 12582912 | tf_op jit(solution)/shard_map/all_to_all | solution.py:29
  365.9 11.2 %copy-start.1 = (bf16[512,2048]{1,0:T(8,128)(2,1)S(1)}, bf16[512,2048]{1,0:T(8,128)(2,1)}, u32[]{:S(2)}) copy-start(bf16[512,2048]{1,0:T(8,128)(2,1)} %param.17) | copy-start | bytes 6291460
  372.4 3.5 copy-start.3
Sparse Core Ops, SparseCore 0:
  33.7 30.8 all-reduce.2
  175.5 26.2 all-gather.1
  230.3 25.5 reduce-scatter.1
where the time goes:
time: 384 us
  waiting for transfers between devices  180 us (47%)
  blocking collectives  84 us (22%)
  local copies, waits for them, and re-layouts  45.7 us (12%)
  matrix products  34.6 us (9%)
  starting transfers between devices  16.6 us (4%)
  between operations  13.4 us (3%)
  other arithmetic  9.89 us (3%)
    all_to_all x1, waiting for transfers between devices, send_back(): lax.all_to_all(result, 'seq', split_axis=0, concat_axis=0, tiled=True)  88.4 us
    all_to_all x1, blocking collectives, shards(): lax.all_to_all(outgoing, 'seq', split_axis=0, concat_axis=0, tiled=True)  84 us
    psum x1, waiting for transfers between devices, shards(): lax.psum(jnp.dot(attended, out_weight, preferred_element_type=jnp.float32...  28 us
    all_gather x1, waiting for transfers between devices, shards(): group = lax.all_gather(inputs, 'exp', axis=0, tiled=True)  26.4 us
    reduce_scatter x1, waiting for transfers between devices, shards(): lax.psum_scatter(jnp.dot(act, w_down[0], preferred_element_type=jnp.float...  25.7 us
    scatter x1, local copies, waits for them, and re-layouts, shards(): outgoing = jnp.zeros((n_experts * capacity, normed.shape[1]), jnp.bfloat1...  24.2 us
    dot_general x1, matrix products, shards(): jnp.dot(act, w_down[0], preferred_element_type=jnp.float32)  18.6 us
    gather x1, local copies, waits for them, and re-layouts, shards(): gathered = back.reshape(n_experts * capacity, back.shape[2])[destination]  10.8 us
  transfers between devices with their start and end apart: 6, of which 6 were waited for; matrix products, arithmetic and copies ran while one was open for 1% of the time, Pallas kernels for 0%

commit v1 on v0

--- a/solution.py
+++ b/solution.py
@@ -98,7 +98,10 @@
     sources = arrived.shape[0]
     slots = arrived.shape[1]
     inputs = arrived.reshape(sources * slots, arrived.shape[2])
-    group = lax.all_gather(inputs, "exp", axis=0, tiled=True)
+    size = lax.axis_size("exp")
+    tiles = jnp.stack([inputs for _ in range(size)])
+    tiles = lax.all_to_all(tiles, "exp", split_axis=0, concat_axis=0)
+    group = jnp.concatenate(tiles, axis=0)
     gate_part = jnp.dot(group, w_gate[0], preferred_element_type=jnp.float32)
     up_part = jnp.dot(group, w_up[0], preferred_element_type=jnp.float32)
     act = (jax.nn.silu(gate_part) * up_part).astype(jnp.bfloat16)

time: 384 us -> 371 us (0.966)
  waiting for transfers between devices: 180 us -> 149 us
  blocking collectives: 84 us -> 97.8 us
  local copies, waits for them, and re-layouts: 45.7 us -> 50.2 us
    all_gather x1 -> x0, waiting for transfers between devices: 26.4 us -> none  [shards(): group = lax.all_gather(inputs, 'exp', axis=0, tiled=True)]
    all_to_all x0 -> x1, blocking collectives: none -> 14 us  [shards(): tiles = lax.all_to_all(tiles, 'exp', split_axis=0, concat_axis=0)]
    unnamed x22 -> x24, local copies, waits for them, and re-layouts: 2.62 us -> 7.1 us
  transfers between devices with their start and end apart: 6 -> 5, of which waited for: 6 -> 5; matrix products, arithmetic and copies ran while one was open for 1% -> 1% of each run, Pallas kernels for 0% -> 0%
where the time goes in v1:
time: 371 us; the launch traced here: 369 us
  waiting for transfers between devices  149 us (40%)
  blocking collectives  97.8 us (26%)
  local copies, waits for them, and re-layouts  50.2 us (14%)
  matrix products  31.2 us (8%)
  starting transfers between devices  16.6 us (4%)
  between operations  13.7 us (4%)
  other arithmetic  11 us (3%)
    all_to_all x1, waiting for transfers between devices, send_back(): lax.all_to_all(result, 'seq', split_axis=0, concat_axis=0, tiled=True)  86.8 us
    all_to_all x1, blocking collectives, shards(): lax.all_to_all(outgoing, 'seq', split_axis=0, concat_axis=0, tiled=True)  83.9 us
    psum x1, waiting for transfers between devices, shards(): lax.psum(jnp.dot(attended, out_weight, preferred_element_type=jnp.float32...  28 us
    scatter x1, local copies, waits for them, and re-layouts, shards(): outgoing = jnp.zeros((n_experts * capacity, normed.shape[1]), jnp.bfloat1...  24.2 us
    reduce_scatter x1, waiting for transfers between devices, shards(): lax.psum_scatter(jnp.dot(act, w_down[0], preferred_element_type=jnp.float...  23 us
    dot_general x1, matrix products, shards(): jnp.dot(act, w_down[0], preferred_element_type=jnp.float32)  18.6 us
    all_to_all x1, blocking collectives, shards(): tiles = lax.all_to_all(tiles, 'exp', split_axis=0, concat_axis=0)  14 us
    gather x1, local copies, waits for them, and re-layouts, shards(): gathered = back.reshape(n_experts * capacity, back.shape[2])[destination]  10.8 us
  transfers between devices with their start and end apart: 5, of which 5 were waited for; matrix products, arithmetic and copies ran while one was open for 1% of the time, Pallas kernels for 0%

profile of v1, /device:TPU:10, one launch (start us, length us, event | category | flops | bytes accessed | tf_op | source)
XLA Modules:
  0.0 369.4 jit_solution(17330567266078570123)
XLA Ops:
  8.9 3.4 collective-permute-start
  12.3 2.4 collective-permute-start.1
  16.6 7.9 %collective-permute-done = bf16[2,256,512]{1,2,0:T(8,128)(2,1)} collective-permute-done((bf16[2,256,512]{1,2,0:T(8,128)(2,1)S(1)}, bf16[2,256,512]{1,2,0:T(8,128)(2,1)}, u32[]{:S(2)}, u32[]{:S(2)}) %collective-permute-start) | collective-permute-done | bytes 524320 | tf_op jit(solution)/shard_map/ppermute | solution.py:19
  24.6 3.1 collective-permute-done.1
  27.7 1.3 pad_maximum_fusion.1
  29.8 1.6 fusion.32
  31.8 1.7 convolution_convert_fusion.1
  34.1 1.8 reduce-window.6
  36.6 28.0 %all-reduce.3.cloned.1.call-done = bf16[256,2048]{1,0:T(8,128)(2,1)} async-done(((bf16[256,2048]{1,0:T(8,128)(2,1)}), bf16[256,2048]{1,0:T(8,128)(2,1)}) %all-reduce.3.cloned.1.call-update) | async-done | bytes 1048592 | tf_op jit(solution)/shard_map/psum | solution.py:73
  64.6 1.3 multiply_reduce_fusion
  65.9 1.3 multiply_convert_fusion
  67.2 24.2 %scatter_custom_fusion = bf16[1536,2048]{1,0:T(8,128)(2,1)} fusion(s32[768]{0:T(1024)S(1)} %fusion.26, bf16[128,2048]{1,0:T(8,128)(2,1)S(1)} %multiply_convert_fusion, s32[1024]{0:T(1024)S(1)} %pad_clamp_fusion.1, bf16[]{:T(256)} %constant.50.clone.1), kind=kCustom, calls=%fused_computation.9 | custom fusion | bytes 6291458 | tf_op jit(solution)/shard_map/scatter | solution.py:94
  91.4 83.9 %all_to_all.15 = bf16[64,24,2048]{2,1,0:T(8,128)(2,1)S(1)} all-to-all(bf16[64,24,2048]{2,1,0:T(8,128)(2,1)} %bitcast.73), channel_id=1, replica_groups=mesh['seq'=64,'exp'=2] {'seq'}, dimensions={0} | all-to-all | bytes 12582912 | tf_op jit(solution)/shard_map/all_to_all | solution.py:97
  176.4 14.0 %all_to_all.16 = bf16[2,1536,2048]{2,1,0:T(8,128)(2,1)S(1)} all-to-all(bf16[2,1536,2048]{2,1,0:T(8,128)(2,1)S(1)} %pad_maximum_fusion), channel_id=1, replica_groups=mesh['seq'=64,'exp'=2] {'exp'}, dimensions={0} | all-to-all | bytes 25165824 | tf_op jit(solution)/shard_map/all_to_all | solution.py:103
  190.4 4.5 %copy-done.2 = bf16[2,1536,2048]{2,1,0:T(8,128)(2,1)} copy-done((bf16[2,1536,2048]{2,1,0:T(8,128)(2,1)}, bf16[2,1536,2048]{2,1,0:T(8,128)(2,1)S(1)}, u32[]{:S(2)}) %copy-start.2) | copy-done | bytes 12582936
  194.9 6.3 %fusion.14 = f32[3072,352]{0,1:T(8,128)} fusion(bf16[3072,2048]{1,0:T(8,128)(2,1)S(1)} %bitcast.75, bf16[1,2048,352]{1,2,0:T(8,128)(2,1)S(1)} %copy-done.9), kind=kOutput, calls=%fused_computation.24 | convolution fusion | flops 4429185024 | bytes 18350080 | tf_op jit(solution)/shard_map/dot_general | solution.py:105
  201.2 18.6 %convolution_convert_fusion = bf16[3072,2048]{1,0:T(8,128)(2,1)} fusion(bf16[3072,2048]{1,0:T(8,128)(2,1)} %bitcast.76, f32[3072,352]{0,1:T(8,128)} %fusion.14, bf16[1,352,2048]{2,1,0:T(8,128)(2,1)} %param.23, bf16[1,2048,352]{1,2,0:T(8,128)(2,1)} %param.22), kind=kOutput, calls=%fused_computation.5 | convolution fusion | flops 8871149568 | bytes 32374784 | tf_op jit(solution)/shard_map/dot_general | solution.py:109
  219.8 23.0 %reduce-scatter.2.cloned.1.call-done = bf16[1536,2048]{1,0:T(8,128)(2,1)} async-done(((bf16[3072,2048]{1,0:T(8,128)(2,1)}), bf16[1536,2048]{1,0:T(8,128)(2,1)}) %reduce-scatter.2.cloned.1.call-update) | async-done | bytes 6291472 | tf_op jit(solution)/shard_map/reduce_scatter | solution.py:108
  242.8 10.7 %all-to-all-start.2 = ((bf16[64,24,2048]{2,1,0:T(8,128)(2,1)}), bf16[64,24,2048]{2,1,0:T(8,128)(2,1)}, u32[]{:S(2)}, u32[]{:S(2)}) async-start(bf16[64,24,2048]{2,1,0:T(8,128)(2,1)} %bitcast.77), calls=%async_computation.3 | async-start | bytes 12582912 | tf_op jit(solution)/shard_map/all_to_all | solution.py:29
  253.7 86.8 %all-to-all-done.2 = bf16[64,24,2048]{2,1,0:T(8,128)(2,1)} async-done(((bf16[64,24,2048]{2,1,0:T(8,128)(2,1)}), bf16[64,24,2048]{2,1,0:T(8,128)(2,1)}, u32[]{:S(2)}, u32[]{:S(2)}) %all-to-all-start.2) | async-done | bytes 6291488 | tf_op jit(solution)/shard_map/all_to_all | solution.py:29
  340.5 10.8 %gather_fusion = bf16[768,2048]{1,0:T(8,128)(2,1)} fusion(bf16[1536,2048]{1,0:T(8,128)(2,1)} %bitcast.15, s32[1024]{0:T(1024)S(1)} %pad_clamp_fusion), kind=kCustom, calls=%fused_computation.1 | custom fusion | bytes 6294528 | tf_op jit(solution)/shard_map/gather | solution.py:116
  351.3 6.4 %reshape.179 = bf16[128,6,2048]{2,1,0:T(8,128)(2,1)} reshape(bf16[768,2048]{1,0:T(8,128)(2,1)} %gather_fusion) | data formatting | bytes 6291456 | tf_op jit(solution)/shard_map/reshape | solution.py:117
  357.7 3.5 fusion.33
  361.3 1.3 fusion.17
  (49 shorter events, 7.9 us)
Async XLA Ops:
  6.5 25.3 %copy-start = (bf16[512,2048]{1,0:T(8,128)(2,1)S(1)}, bf16[512,2048]{1,0:T(8,128)(2,1)}, u32[]{:S(2)}) copy-start(bf16[512,2048]{1,0:T(8,128)(2,1)} %param.17) | copy-start | bytes 6291460
  6.5 58.0 %all-reduce.3.cloned.1.call-start = ((), (), s32[]{:S(2)}) async-start(), calls=%async_computation.4 | async-start | bytes 2097152 | tf_op jit(solution)/shard_map/psum | solution.py:73
  8.9 15.7 %collective-permute-start = (bf16[2,256,512]{1,2,0:T(8,128)(2,1)S(1)}, bf16[2,256,512]{1,2,0:T(8,128)(2,1)}, u32[]{:S(2)}, u32[]{:S(2)}) collective-permute-start(bf16[2,256,512]{1,2,0:T(8,128)(2,1)S(1)} %pad_maximum_fusion.2), channel_id=1, source_target_pairs={{0,2},{2,4},{4,6},{6,8},{8,10},{10,12},{12,14},{14,16},{16,18},{18... | collective-permute-start | bytes 1572872 | tf_op jit(solution)/shard_map/ppermute | solution.py:19
  12.3 15.4 %collective-permute-start.1 = (bf16[2,256,512]{1,2,0:T(8,128)(2,1)S(1)}, bf16[2,256,512]{1,2,0:T(8,128)(2,1)}, u32[]{:S(2)}, u32[]{:S(2)}) collective-permute-start(bf16[2,256,512]{1,2,0:T(8,128)(2,1)S(1)} %pad_maximum_fusion.2), channel_id=1, source_target_pairs={{2,0},{4,2},{6,4},{8,6},{10,8},{12,10},{14,12},{16,14},{18,16},{20... | collective-permute-start | bytes 1572872 | tf_op jit(solution)/shard_map/ppermute | solution.py:21
  16.6 12.5 %copy-start.5 = (bf16[256,512]{1,0:T(8,128)(2,1)S(1)}, bf16[256,512]{1,0:T(8,128)(2,1)}, u32[]{:S(2)}) copy-start(bf16[256,512]{1,0:T(8,128)(2,1)} %param.12) | copy-start | bytes 786436
  31.8 1.9 copy-start.6
  31.8 32.8 %copy-start.3 = (bf16[128,2048]{1,0:T(8,128)(2,1)S(1)}, bf16[128,2048]{1,0:T(8,128)(2,1)}, u32[]{:S(2)}) copy-start(bf16[128,2048]{1,0:T(8,128)(2,1)} %param.15) | copy-start | bytes 1572868
  31.8 34.1 %copy-start.7 = (f32[2048]{0:T(1024)S(1)}, f32[2048]{0:T(1024)}, u32[]{:S(2)}) copy-start(f32[2048]{0:T(1024)} %param.18) | copy-start | bytes 24580
  33.6 209.3 %reduce-scatter.2.cloned.1.call-start = ((), (), s32[]{:S(2)}) async-start(), calls=%async_computation.5 | async-start | bytes 18874368 | tf_op jit(solution)/shard_map/reduce_scatter | solution.py:108
  176.4 18.5 %copy-start.9 = (bf16[1,2048,352]{1,2,0:T(8,128)(2,1)S(1)}, bf16[1,2048,352]{1,2,0:T(8,128)(2,1)}, u32[]{:S(2)}) copy-start(bf16[1,2048,352]{1,2,0:T(8,128)(2,1)} %param.21) | copy-start | bytes 4325380
  190.4 4.5 %copy-start.2 = (bf16[2,1536,2048]{2,1,0:T(8,128)(2,1)}, bf16[2,1536,2048]{2,1,0:T(8,128)(2,1)S(1)}, u32[]{:S(2)}) copy-start(bf16[2,1536,2048]{2,1,0:T(8,128)(2,1)S(1)} %all_to_all.16) | copy-start | bytes 37748740
  242.8 10.7 %copy-start.8 = (f32[128,6]{0,1:T(8,128)S(1)}, f32[128,6]{0,1:T(8,128)}, u32[]{:S(2)}) copy-start(f32[128,6]{0,1:T(8,128)} %param.20) | copy-start | bytes 9220
  242.8 97.7 %all-to-all-start.2 = ((bf16[64,24,2048]{2,1,0:T(8,128)(2,1)}), bf16[64,24,2048]{2,1,0:T(8,128)(2,1)}, u32[]{:S(2)}, u32[]{:S(2)}) async-start(bf16[64,24,2048]{2,1,0:T(8,128)(2,1)} %bitcast.77), calls=%async_computation.3 | async-start | bytes 12582912 | tf_op jit(solution)/shard_map/all_to_all | solution.py:29
  351.3 11.2 %copy-start.1 = (bf16[512,2048]{1,0:T(8,128)(2,1)S(1)}, bf16[512,2048]{1,0:T(8,128)(2,1)}, u32[]{:S(2)}) copy-start(bf16[512,2048]{1,0:T(8,128)(2,1)} %param.17) | copy-start | bytes 6291460
  357.7 3.5 copy-start.4
Sparse Core Ops, SparseCore 0:
  33.7 30.8 all-reduce.2
  220.0 22.8 reduce-scatter.1
